TPU v7x, 128 devices: a whole 4x4x4 slice. The times are simulated.
128 devices in a mesh: row: 8 (over x, core), col: 16 (over y, z).
Axes of the slice: x: 4, y: 4, z: 4, core: 2. Of those that a mesh axis runs over, the one named last changes fastest.
Arguments:
- density_factor: bfloat16 [524288, 256], P(('row', 'col'))
- onsite: float32 [524288], P(('row', 'col')), may hold values from -4 to 4
- neighbour_ids: int32 [1024, 8], P(('row', 'col')), may hold values from 0 to 1023, as said below
- neighbour_count: int32 [1024], P(('row', 'col')), may hold values from 1 to 8, as said below
- coupling_type: int32 [1024, 8], P(('row', 'col')), may hold values from 0 to 3
- coupling_blocks: bfloat16 [4, 512, 512], replicated, may hold values from -0.25 to 0.25
- bath_pattern: int32 [1024], P(('row', 'col')), may hold values from 0 to 3
- bath_blocks: bfloat16 [4, 512, 512], replicated, may hold values from -0.25 to 0.25
Outputs:
- new_factor: bfloat16 [524288, 256], P(('row', 'col'))
Inputs may be any that keep to these rules, and one draw needn't show every extreme that they name: `neighbour_ids`: every neighbour of block b lies among the 128 blocks that share b's index of row, at most half of 128 blocks from b when that group is taken as a loop, and is never b itself; some block has a neighbour exactly half of 128 blocks away. Only the first neighbour_count[b] slots of block b's lists are used; some block uses all 8.
All inputs are finite; a program needn't handle non-finite values.
Results may differ from a plain program's by a relative error of at most 0.0056.
Values may be sent and summed in bfloat16 or wider, within the bound.
A program may use at most 192 MiB of HBM per device.

v0:
```python
import jax
import jax.numpy as jnp
from jax import lax
from jax.sharding import PartitionSpec as P

SWEEPS = 2
time_step = 0.25


def orthonormal_steps(gram, rank_cols):
    basis = jnp.eye(2 * rank_cols, rank_cols, dtype=jnp.float32)
    for sweep in range(SWEEPS):
        image = jnp.dot(gram, basis, precision=lax.Precision.HIGHEST)
        inner = jnp.dot(image.T, image, precision=lax.Precision.HIGHEST)
        factor = jnp.linalg.cholesky(inner)
        basis = lax.linalg.triangular_solve(
            factor, image, left_side=False, lower=True, transpose_a=True
        )
    return basis


def shards(
    density_factor,
    onsite,
    neighbour_ids,
    neighbour_count,
    coupling_type,
    coupling_blocks,
    bath_pattern,
    bath_blocks,
):
    blocks, slots = neighbour_ids.shape
    kinds = coupling_blocks.shape[0]
    block_rows = coupling_blocks.shape[1]
    rank_cols = density_factor.shape[1]
    col_count = lax.axis_size("col")
    group_blocks = col_count * blocks
    row_place = lax.axis_index("row")
    in_group = neighbour_ids - row_place * group_blocks
    slot_live = jnp.arange(slots, dtype=jnp.int32)[None, :] < neighbour_count[:, None]
    kind_match = (
        coupling_type[:, :, None] == jnp.arange(kinds, dtype=jnp.int32)[None, None, :]
    ) & slot_live[:, :, None]
    kind_float = kind_match.astype(jnp.float32)
    gathered = lax.all_gather(density_factor, "col", axis=0, tiled=True)
    hits = (
        in_group[:, :, None] == jnp.arange(group_blocks, dtype=jnp.int32)[None, None, :]
    ).astype(jnp.float32)
    mixing = jnp.einsum("bkt,bkn->btn", kind_float, hits).astype(jnp.bfloat16)
    flat_blocks = gathered.reshape(group_blocks, block_rows * rank_cols)
    summed = jnp.einsum("btn,nm->btm", mixing, flat_blocks, preferred_element_type=jnp.float32)
    summed = summed.reshape(blocks, kinds, block_rows, rank_cols).astype(jnp.bfloat16)
    coupled = jnp.einsum(
        "tij,btjr->bir", coupling_blocks, summed, preferred_element_type=jnp.float32
    )
    own_rows = density_factor.reshape(blocks, block_rows, rank_cols)
    bath_pick = bath_blocks[bath_pattern]
    bathed = jnp.einsum(
        "bij,bjr->bir", bath_pick, own_rows, preferred_element_type=jnp.float32
    ).astype(jnp.bfloat16)
    factor_wide = own_rows.astype(jnp.float32)
    energy = onsite.reshape(blocks, block_rows, 1)
    moved = (factor_wide - time_step * (energy * factor_wide + coupled)).astype(jnp.bfloat16)
    stacked = jnp.concatenate([moved, bathed], axis=2).reshape(blocks * block_rows, 2 * rank_cols)
    local_gram = lax.dot_general(
        stacked, stacked, (((0,), (0,)), ((), ())), preferred_element_type=jnp.float32
    )
    gram_sum = lax.psum(local_gram, ("row", "col"))
    rotation = orthonormal_steps(gram_sum, rank_cols).astype(jnp.bfloat16)
    return jnp.dot(stacked, rotation, preferred_element_type=jnp.float32).astype(jnp.bfloat16)


def solution(mesh):
    placed = (
        P(("row", "col"), None),
        P(("row", "col")),
        P(("row", "col"), None),
        P(("row", "col")),
        P(("row", "col"), None),
        P(),
        P(("row", "col")),
        P(),
    )
    return jax.shard_map(
        shards, mesh=mesh, in_specs=placed, out_specs=P(("row", "col"), None), check_vma=False
    )
```

profile of v0, /device:TPU:1, one launch (start us, length us, event | category | flops | bytes accessed | tf_op | source)
XLA Modules:
  0.0 618.0 jit_solution(14788270948122039171)
XLA Ops:
  8.0 3.9 copy.12
  12.0 2.9 gather_fusion
  14.9 4.2 convolution_convert_fusion.1
  19.1 190.8 %all-gather.2.cloned.1.call-done = bf16[65536,256]{1,0:T(8,128)(2,1)} async-done(((bf16[4096,256]{1,0:T(8,128)(2,1)}), bf16[65536,256]{1,0:T(8,128)(2,1)}) %all-gather.2.cloned.1.call-update) | async-done | bytes 33554448 | tf_op jit(solution)/shard_map/all_gather | solution.py:45
  210.0 33.2 %reshape.54 = bf16[128,131072]{1,0:T(8,128)(2,1)} reshape(bf16[65536,256]{1,0:T(8,128)(2,1)} %all-gather.2.cloned.1.call-done) | data formatting | bytes 67108864 | tf_op jit(solution)/shard_map/reshape | solution.py:50
  243.2 23.1 %copy.24 = bf16[16,8,512,256]{3,2,1,0:T(8,128)(2,1)} copy(bf16[16,8,512,256]{3,1,2,0:T(8,128)(2,1)} %bitcast.98) | data formatting | bytes 67108864
  266.2 36.0 %fusion = bf16[8,4,512,256]{3,1,2,0:T(4,128)(2,1)} fusion(bf16[512,256,128,1]{1,0,2,3:T(8,128)(2,1)} %bitcast.99, s32[8,8]{1,0:T(8,128)S(1)} %broadcast_subtract_fusion, s32[8,8]{1,0:T(8,128)S(1)} %copy-done.5, pred[8,8]{1,0:T(8,128)(4,1)S(1)} %iota_compare_fusion.9), kind=kOutput, calls=%fused_computation.5 | convolution fusion | flops 1073820160 | bytes 41943616 | tf_op jit(solution)/shard_map/btn,nm->btm/dot_general | solution.py:51
  302.3 13.8 %copy.20 = bf16[8,4,512,256]{2,3,1,0:T(8,128)(2,1)} copy(bf16[8,4,512,256]{3,1,2,0:T(4,128)(2,1)} %fusion) | data formatting | bytes 16777216 | tf_op jit(solution)/shard_map/btn,nm->btm/dot_general | solution.py:51
  316.1 9.6 %fusion.6 = bf16[8,512,256]{1,2,0:T(8,128)(2,1)S(1)} fusion(bf16[8,512,256]{1,2,0:T(8,128)(2,1)} %copy.12, bf16[8,4,512,256]{2,3,1,0:T(8,128)(2,1)} %copy.20, bf16[4,512,512]{2,1,0:T(8,128)(2,1)} %param.16, f32[8,512]{1,0:T(8,128)S(1)} %mul.19), kind=kOutput, calls=%fused_computation.14 | convolution fusion | flops 4301258752 | bytes 14696448 | tf_op jit(solution)/shard_map/tij,btjr->bir/dot_general | solution.py:53
  325.7 1.3 copy-done.3
  327.0 3.3 convolution_bitcast_fusion
  330.3 3.8 pad_maximum_fusion
  334.2 6.5 %copy.14 = bf16[8,512,512]{2,1,0:T(8,128)(2,1)} copy(bf16[8,512,512]{1,2,0:T(8,128)(2,1)} %pad_maximum_fusion) | data formatting | bytes 8388608 | tf_op jit(solution)/shard_map/concatenate | solution.py:64
  340.6 136.9 %all-reduce.3.cloned.1.call-done = f32[512,512]{1,0:T(8,128)} async-done(((f32[512,512]{1,0:T(8,128)}), f32[512,512]{1,0:T(8,128)}) %all-reduce.3.cloned.1.call-update) | async-done | bytes 1048592 | tf_op jit(solution)/shard_map/psum | solution.py:68
  477.5 1.9 fusion.15
  479.4 1.0 fusion.49
  480.7 11.7 %cholesky.130 = f32[128,128]{1,0:T(8,128)S(1)} custom-call(f32[128,128]{1,0:T(8,128)S(1)} %cholesky.194), custom_call_target="Cholesky" | custom-call | tf_op jit(solution)/shard_map/jit(cholesky)/cholesky | solution.py:15
  492.4 9.8 %custom-call.13 = f32[1,128,128]{1,2,0:T(8,128)S(1)} custom-call(f32[1,128,128]{2,1,0:T(8,128)S(1)} %get-tuple-element.50), custom_call_target="InvertDiagBlocksLowerTriangular" | custom-call | tf_op jit(solution)/shard_map/jit(cholesky)/cholesky | solution.py:15
  502.7 11.7 %cholesky.147 = f32[128,128]{1,0:T(8,128)S(1)} custom-call(f32[128,128]{1,0:T(8,128)S(1)} %convolution_subtract_fusion.3), custom_call_target="Cholesky" | custom-call | tf_op jit(solution)/shard_map/jit(cholesky)/cholesky | solution.py:15
  516.6 4.0 while.4
  517.2 1.4 bitcast_dynamic-update-slice_fusion.4
  519.2 1.4 bitcast_dynamic-update-slice_fusion.4
  520.6 20.1 %custom-call.14 = f32[2,128,128]{1,2,0:T(8,128)S(1)} custom-call(f32[2,128,128]{2,1,0:T(8,128)S(1)} %get-tuple-element.21), custom_call_target="InvertDiagBlocksLowerTriangular" | custom-call | tf_op jit(solution)/shard_map/triangular_solve/custom-call.0 | solution.py:16
  543.1 1.0 fusion.50
  544.3 11.7 %cholesky.164 = f32[128,128]{1,0:T(8,128)S(1)} custom-call(f32[128,128]{1,0:T(8,128)S(1)} %cholesky.197), custom_call_target="Cholesky" | custom-call | tf_op jit(solution)/shard_map/jit(cholesky)/cholesky | solution.py:15
  556.7 9.8 %custom-call.15 = f32[1,128,128]{1,2,0:T(8,128)S(1)} custom-call(f32[1,128,128]{2,1,0:T(8,128)S(1)} %get-tuple-element.46), custom_call_target="InvertDiagBlocksLowerTriangular" | custom-call | tf_op jit(solution)/shard_map/jit(cholesky)/cholesky | solution.py:15
  567.1 11.9 %cholesky.181 = f32[128,128]{1,0:T(8,128)S(1)} custom-call(f32[128,128]{1,0:T(8,128)S(1)} %convolution_subtract_fusion.2), custom_call_target="Cholesky" | custom-call | tf_op jit(solution)/shard_map/jit(cholesky)/cholesky | solution.py:15
  580.9 3.9 while.5
  581.5 1.4 bitcast_dynamic-update-slice_fusion.5
  583.5 1.4 bitcast_dynamic-update-slice_fusion.5
  584.9 19.7 %custom-call.16 = f32[2,128,128]{1,2,0:T(8,128)S(1)} custom-call(f32[2,128,128]{2,1,0:T(8,128)S(1)} %get-tuple-element.22), custom_call_target="InvertDiagBlocksLowerTriangular" | custom-call | tf_op jit(solution)/shard_map/triangular_solve/custom-call.0 | solution.py:16
  606.0 4.9 convolution_convert_fusion
  (64 shorter events, 11.4 us)
Async XLA Ops:
  6.5 5.4 copy-start
  6.5 5.4 copy-start.6
  6.5 203.4 %all-gather.2.cloned.1.call-start = ((), (), s32[]{:S(2)}) async-start(), calls=%async_computation | async-start | bytes 35651584 | tf_op jit(solution)/shard_map/all_gather | solution.py:45
  7.3 470.3 %all-reduce.3.cloned.1.call-start = ((), (), s32[]{:S(2)}) async-start(), calls=%async_computation.1 | async-start | bytes 2097152 | tf_op jit(solution)/shard_map/psum | solution.py:68
  12.0 2.9 copy-start.7
  12.0 3.0 copy-start.4
  243.2 23.1 %copy-start.5 = (s32[8,8]{1,0:T(8,128)S(1)}, s32[8,8]{1,0:T(8,128)}, u32[]{:S(2)}) copy-start(s32[8,8]{1,0:T(8,128)} %param.15) | copy-start | bytes 772
  325.6 1.3 copy-start.3
  477.5 64.6 %copy-start.2 = (f32[512,512]{1,0:T(8,128)S(1)}, f32[512,512]{1,0:T(8,128)}, u32[]{:S(2)}) copy-start(f32[512,512]{1,0:T(8,128)} %all-reduce.3.cloned.1.call-done) | copy-start | bytes 3145732
  606.0 5.0 copy-start.1
Sparse Core Ops, SparseCore 0:
  9.5 200.4 all-gather.1
  330.4 147.0 all-reduce.2
where the time goes:
time: 623 us; the launch traced here: 618 us
  waiting for transfers between devices  328 us (53%)
  other arithmetic  113 us (18%)
  local copies, waits for them, and re-layouts  93.6 us (15%)
  matrix products  66.8 us (11%)
  between operations  16.5 us (3%)
    all_gather x1, waiting for transfers between devices, shards(): gathered = lax.all_gather(density_factor, 'col', axis=0, tiled=True)  191 us
    psum x1, waiting for transfers between devices, shards(): gram_sum = lax.psum(local_gram, ('row', 'col'))  137 us
    another operation x13, other arithmetic, orthonormal_steps(): factor = jnp.linalg.cholesky(inner)  68.8 us
    another operation x5, other arithmetic, orthonormal_steps(): lax.linalg.triangular_solve(factor, image, left_side=False, lower=True, t...  39.8 us
    dot_general x1, matrix products, shards(): jnp.einsum('btn,nm->btm', mixing, flat_blocks, preferred_element_type=jnp...  36 us
    reshape x1, local copies, waits for them, and re-layouts, shards(): flat_blocks = gathered.reshape(group_blocks, block_rows * rank_cols)  33.2 us
    unnamed x17, local copies, waits for them, and re-layouts  24.4 us
    dot_general x1, local copies, waits for them, and re-layouts, shards(): jnp.einsum('btn,nm->btm', mixing, flat_blocks, preferred_element_type=jnp...  13.8 us
  transfers between devices with their start and end apart: 2, of which 2 were waited for; matrix products, arithmetic and copies ran while one was open for 4% of the time, Pallas kernels for 0%

commit v1 on v0

--- a/solution.py
+++ b/solution.py
@@ -65,7 +65,8 @@
     local_gram = lax.dot_general(
         stacked, stacked, (((0,), (0,)), ((), ())), preferred_element_type=jnp.float32
     )
-    gram_sum = lax.psum(local_gram, ("row", "col"))
+    parts = lax.all_gather(local_gram, ("row", "col"), axis=0, tiled=False)
+    gram_sum = parts.sum(axis=0)
     rotation = orthonormal_steps(gram_sum, rank_cols).astype(jnp.bfloat16)
     return jnp.dot(stacked, rotation, preferred_element_type=jnp.float32).astype(jnp.bfloat16)
 

time: 623 us -> 798 us (1.28)
  waiting for transfers between devices: 328 us -> 466 us
  other arithmetic: 113 us -> 153 us
    all_gather x0 -> x1, waiting for transfers between devices: none -> 273 us  [shards(): parts = lax.all_gather(local_gram, ('row', 'col'), axis=0, tiled=False)]
    psum x1 -> x0, waiting for transfers between devices: 137 us -> none  [shards(): gram_sum = lax.psum(local_gram, ('row', 'col'))]
    reduce_sum x0 -> x1, other arithmetic: none -> 40.8 us  [shards(): gram_sum = parts.sum(axis=0)]
  transfers between devices with their start and end apart: 2 -> 2, of which waited for: 2 -> 2; matrix products, arithmetic and copies ran while one was open for 4% -> 3% of each run, Pallas kernels for 0% -> 0%
where the time goes in v1:
time: 798 us; the launch traced here: 794 us
  waiting for transfers between devices  466 us (58%)
  other arithmetic  153 us (19%)
  local copies, waits for them, and re-layouts  92.8 us (12%)
  matrix products  65.6 us (8%)
  between operations  16.5 us (2%)
    all_gather x1, waiting for transfers between devices, shards(): parts = lax.all_gather(local_gram, ('row', 'col'), axis=0, tiled=False)  273 us
    all_gather x1, waiting for transfers between devices, shards(): gathered = lax.all_gather(density_factor, 'col', axis=0, tiled=True)  192 us
    another operation x13, other arithmetic, orthonormal_steps(): factor = jnp.linalg.cholesky(inner)  68.7 us
    reduce_sum x1, other arithmetic, shards(): gram_sum = parts.sum(axis=0)  40.8 us
    another operation x5, other arithmetic, orthonormal_steps(): lax.linalg.triangular_solve(factor, image, left_side=False, lower=True, t...  39.8 us
    dot_general x1, matrix products, shards(): jnp.einsum('btn,nm->btm', mixing, flat_blocks, preferred_element_type=jnp...  36 us
    reshape x1, local copies, waits for them, and re-layouts, shards(): flat_blocks = gathered.reshape(group_blocks, block_rows * rank_cols)  33.2 us
    unnamed x17, local copies, waits for them, and re-layouts  24.4 us
  transfers between devices with their start and end apart: 2, of which 2 were waited for; matrix products, arithmetic and copies ran while one was open for 3% of the time, Pallas kernels for 0%

profile of v1, /device:TPU:1, one launch (start us, length us, event | category | flops | bytes accessed | tf_op | source)
XLA Modules:
  0.0 793.9 jit_solution(13330452660732497303)
XLA Ops:
  7.3 3.9 copy.12
  11.3 2.9 gather_fusion
  14.3 4.2 convolution_convert_fusion.1
  18.4 191.5 %all-gather.4.cloned.1.call-done = bf16[65536,256]{1,0:T(8,128)(2,1)} async-done(((bf16[4096,256]{1,0:T(8,128)(2,1)}), bf16[65536,256]{1,0:T(8,128)(2,1)}) %all-gather.4.cloned.1.call-update) | async-done | bytes 33554448 | tf_op jit(solution)/shard_map/all_gather | solution.py:45
  210.0 33.2 %reshape.54 = bf16[128,131072]{1,0:T(8,128)(2,1)} reshape(bf16[65536,256]{1,0:T(8,128)(2,1)} %all-gather.4.cloned.1.call-done) | data formatting | bytes 67108864 | tf_op jit(solution)/shard_map/reshape | solution.py:50
  243.2 23.1 %copy.24 = bf16[16,8,512,256]{3,2,1,0:T(8,128)(2,1)} copy(bf16[16,8,512,256]{3,1,2,0:T(8,128)(2,1)} %bitcast.99) | data formatting | bytes 67108864
  266.2 36.0 %fusion = bf16[8,4,512,256]{3,1,2,0:T(4,128)(2,1)} fusion(bf16[512,256,128,1]{1,0,2,3:T(8,128)(2,1)} %bitcast.100, s32[8,8]{1,0:T(8,128)S(1)} %broadcast_subtract_fusion, s32[8,8]{1,0:T(8,128)S(1)} %copy-done.5, pred[8,8]{1,0:T(8,128)(4,1)S(1)} %iota_compare_fusion.9), kind=kOutput, calls=%fused_computation.5 | convolution fusion | flops 1073820160 | bytes 41943616 | tf_op jit(solution)/shard_map/btn,nm->btm/dot_general | solution.py:51
  302.3 13.8 %copy.20 = bf16[8,4,512,256]{2,3,1,0:T(8,128)(2,1)} copy(bf16[8,4,512,256]{3,1,2,0:T(4,128)(2,1)} %fusion) | data formatting | bytes 16777216 | tf_op jit(solution)/shard_map/btn,nm->btm/dot_general | solution.py:51
  316.1 9.6 %fusion.6 = bf16[8,512,256]{1,2,0:T(8,128)(2,1)S(1)} fusion(bf16[8,512,256]{1,2,0:T(8,128)(2,1)} %copy.12, bf16[8,4,512,256]{2,3,1,0:T(8,128)(2,1)} %copy.20, bf16[4,512,512]{2,1,0:T(8,128)(2,1)} %param.16, f32[8,512]{1,0:T(8,128)S(1)} %mul.19), kind=kOutput, calls=%fused_computation.14 | convolution fusion | flops 4301258752 | bytes 14696448 | tf_op jit(solution)/shard_map/tij,btjr->bir/dot_general | solution.py:53
  325.7 1.3 copy-done.2
  327.0 3.4 convolution_bitcast_fusion
  330.4 3.8 pad_maximum_fusion
  334.3 6.5 copy.14
  340.7 273.3 %all-gather.6.cloned.1.call-done = f32[65536,512]{1,0:T(8,128)} async-done(((f32[512,512]{1,0:T(8,128)}), f32[65536,512]{1,0:T(8,128)}) %all-gather.6.cloned.1.call-update) | async-done | bytes 134217744 | tf_op jit(solution)/shard_map/all_gather | solution.py:68
  614.1 40.8 %reduce_sum.9 = f32[512,512]{1,0:T(8,128)S(1)} reduce(f32[128,512,512]{2,1,0:T(8,128)} %bitcast.10, f32[]{:T(128)} %constant.70.clone.1), dimensions={0}, to_apply=%region_0.0 | reduce | flops 33292288 | bytes 135266304 | tf_op jit(solution)/shard_map/reduce_sum | solution.py:69
  655.4 1.0 fusion.49
  656.6 11.7 %cholesky.130 = f32[128,128]{1,0:T(8,128)S(1)} custom-call(f32[128,128]{1,0:T(8,128)S(1)} %cholesky.194), custom_call_target="Cholesky" | custom-call | tf_op jit(solution)/shard_map/jit(cholesky)/cholesky | solution.py:15
  668.4 9.8 %custom-call.13 = f32[1,128,128]{1,2,0:T(8,128)S(1)} custom-call(f32[1,128,128]{2,1,0:T(8,128)S(1)} %get-tuple-element.50), custom_call_target="InvertDiagBlocksLowerTriangular" | custom-call | tf_op jit(solution)/shard_map/jit(cholesky)/cholesky | solution.py:15
  678.7 11.7 %cholesky.147 = f32[128,128]{1,0:T(8,128)S(1)} custom-call(f32[128,128]{1,0:T(8,128)S(1)} %convolution_subtract_fusion.3), custom_call_target="Cholesky" | custom-call | tf_op jit(solution)/shard_map/jit(cholesky)/cholesky | solution.py:15
  692.5 4.0 while.4
  693.1 1.4 bitcast_dynamic-update-slice_fusion.4
  695.1 1.4 bitcast_dynamic-update-slice_fusion.4
  696.5 20.1 %custom-call.14 = f32[2,128,128]{1,2,0:T(8,128)S(1)} custom-call(f32[2,128,128]{2,1,0:T(8,128)S(1)} %get-tuple-element.21), custom_call_target="InvertDiagBlocksLowerTriangular" | custom-call | tf_op jit(solution)/shard_map/triangular_solve/custom-call.0 | solution.py:16
  719.0 1.0 fusion.50
  720.3 11.7 %cholesky.164 = f32[128,128]{1,0:T(8,128)S(1)} custom-call(f32[128,128]{1,0:T(8,128)S(1)} %cholesky.197), custom_call_target="Cholesky" | custom-call | tf_op jit(solution)/shard_map/jit(cholesky)/cholesky | solution.py:15
  732.0 9.8 %custom-call.15 = f32[1,128,128]{1,2,0:T(8,128)S(1)} custom-call(f32[1,128,128]{2,1,0:T(8,128)S(1)} %get-tuple-element.46), custom_call_target="InvertDiagBlocksLowerTriangular" | custom-call | tf_op jit(solution)/shard_map/jit(cholesky)/cholesky | solution.py:15
  742.3 11.8 %cholesky.181 = f32[128,128]{1,0:T(8,128)S(1)} custom-call(f32[128,128]{1,0:T(8,128)S(1)} %convolution_subtract_fusion.2), custom_call_target="Cholesky" | custom-call | tf_op jit(solution)/shard_map/jit(cholesky)/cholesky | solution.py:15
  756.8 4.0 while.5
  757.4 1.4 bitcast_dynamic-update-slice_fusion.5
  759.4 1.4 bitcast_dynamic-update-slice_fusion.5
  760.8 19.7 %custom-call.16 = f32[2,128,128]{1,2,0:T(8,128)S(1)} custom-call(f32[2,128,128]{2,1,0:T(8,128)S(1)} %get-tuple-element.22), custom_call_target="InvertDiagBlocksLowerTriangular" | custom-call | tf_op jit(solution)/shard_map/triangular_solve/custom-call.0 | solution.py:16
  781.9 4.9 convolution_convert_fusion
  (65 shorter events, 11.3 us)
Async XLA Ops:
  6.5 4.7 copy-start
  6.5 4.7 copy-start.3
  6.5 4.7 copy-start.6
  6.5 203.4 %all-gather.4.cloned.1.call-start = ((), (), s32[]{:S(2)}) async-start(), calls=%async_computation | async-start | bytes 35651584 | tf_op jit(solution)/shard_map/all_gather | solution.py:45
  7.3 606.8 %all-gather.6.cloned.1.call-start = ((), (), s32[]{:S(2)}) async-start(), calls=%async_computation.1 | async-start | bytes 135266304 | tf_op jit(solution)/shard_map/all_gather | solution.py:68
  11.3 2.9 copy-start.7
  11.3 3.0 copy-start.4
  243.2 23.1 %copy-start.5 = (s32[8,8]{1,0:T(8,128)S(1)}, s32[8,8]{1,0:T(8,128)}, u32[]{:S(2)}) copy-start(s32[8,8]{1,0:T(8,128)} %param.15) | copy-start | bytes 772
  325.6 1.3 copy-start.2
  781.9 5.0 copy-start.1
Sparse Core Ops, SparseCore 0:
  9.5 200.4 all-gather.3
  330.5 283.4 all-gather.5
